TPU v7x, 128 devices: a whole 4x4x4 slice. The times are simulated.
128 devices in a mesh: tm: 16 (over x, y), sector: 8 (over z, core).
Axes of the slice: x: 4, y: 4, z: 4, core: 2. Of those that a mesh axis runs over, the one named last changes fastest.
Arguments:
- propagator: bfloat16 [8, 16, 640, 640], P('sector', 'tm'), may hold values from -6 to 6
- rising_op: bfloat16 [8, 640, 640], P('sector'), may hold values from -0.25 to 0.25
- energies: float32 [8, 640], P('sector'), may hold values from 0.5 to 40
- hyb_particle: float32 [16], P('tm'), may hold values from 0.2 to 1
- hyb_hole: float32 [16], P('tm'), may hold values from 0.2 to 1
- sector_sizes: int32 [8], P('sector'), may hold values from 160 to 640, as said below
Outputs:
- new_prop: bfloat16 [8, 16, 640, 640], P('sector', 'tm')
Inputs may be any that keep to these rules, and one draw needn't show every extreme that they name: `sector_sizes`: one sector holds exactly 640 states.
All inputs are finite; a program needn't handle non-finite values.
Results may differ from a plain program's by a relative error of at most 0.0061.
Values may be sent and summed in bfloat16 or wider, within the bound.
No kernel may reach another device: no remote copies, remote signals or barrier semaphores. Data moves between devices by JAX's collectives and lax.ppermute only.
A program may use at most 128 MiB of HBM per device.

v0:
```python
import jax
import jax.numpy as jnp
from jax import lax
from jax.sharding import PartitionSpec as P


def shifted(block, axis, distance):
    devices = range(lax.axis_size(axis))
    route = [(i - distance, i) for i in devices if i - distance in devices]
    return lax.ppermute(block, axis, route)


def split_up(value, dim, size):
    before, after = (value.shape[:dim], value.shape[dim + 1 :])
    return jnp.moveaxis(value.reshape(*before, size, -1, *after), dim, 0)


def piece_ends(length, count):
    step = length // count
    if step >= 8:
        step -= step % 8
    return [step * k for k in range(1, count)]


def laid_out(pieces, dim):
    dims = list(pieces.shape[1:])
    dims[dim] *= pieces.shape[0]
    return jnp.moveaxis(pieces, 0, dim).reshape(dims)


def several_exchanges(value, axis, pieces, split_dim, concat_dim):
    blocks = split_up(value, split_dim, lax.axis_size(axis))
    cut = max(range(1, max(2, blocks.ndim - 1)), key=lambda d: blocks.shape[d])
    finished = []
    for share in jnp.split(blocks, piece_ends(blocks.shape[cut], pieces), axis=cut):
        if share.size:
            finished.append(lax.all_to_all(share, axis, split_axis=0, concat_axis=0, tiled=True))
    return laid_out(jnp.concatenate(finished, axis=cut), concat_dim)


def per_device(propagator, rising_op, energies, hyb_particle, hyb_hole, sector_sizes):
    t_dev = propagator.shape[1]
    states = propagator.shape[2]
    time_count = t_dev * lax.axis_size("tm")
    step_size = 1.0 / time_count
    positions = jnp.arange(states, dtype=jnp.int32)
    live_mask = positions < sector_sizes[0]
    square = live_mask[:, None] & live_mask[None, :]
    masked_prop = jnp.where(square[None], propagator[0], jnp.zeros((), jnp.bfloat16))
    operator = rising_op[0]
    raised = jnp.einsum(
        "ik,tkl->til", operator, masked_prop, preferred_element_type=jnp.float32
    ).astype(jnp.bfloat16)
    upward = jnp.einsum("tik,jk->tij", raised, operator, preferred_element_type=jnp.float32).astype(
        jnp.bfloat16
    )
    from_below = shifted(upward, "sector", 1)
    from_above = shifted(masked_prop, "sector", -1)
    lowered = jnp.einsum(
        "ki,tkl->til", operator, from_above, preferred_element_type=jnp.float32
    ).astype(jnp.bfloat16)
    downward = jnp.einsum("tik,kl->til", lowered, operator, preferred_element_type=jnp.float32)
    combined = (
        hyb_particle[:, None, None] * from_below.astype(jnp.float32)
        + hyb_hole[:, None, None] * downward
    )
    self_energy = jnp.where(square[None], combined, jnp.zeros((), jnp.float32)).astype(jnp.bfloat16)
    rows_each = states // lax.axis_size("tm")
    first_row = lax.axis_index("tm") * rows_each
    lag_rows = several_exchanges(self_energy, "tm", 2, 1, 0)
    history = lax.all_gather(masked_prop, "tm", axis=0, tiled=True)
    mirrored = jnp.concatenate([history[::-1], history], 0)
    slots = jnp.arange(time_count, dtype=jnp.int32)
    wide_slots = jnp.arange(time_count + 1, dtype=jnp.int32)

    def pair_step(lag, sums):
        forward, backward = sums
        other = time_count - 1 - lag
        window = lax.dynamic_slice_in_dim(mirrored, lag, time_count + 1, 0)
        near = lax.dynamic_index_in_dim(lag_rows, lag, 0, keepdims=False)
        far = lax.dynamic_index_in_dim(lag_rows, other, 0, keepdims=False)
        left = jnp.where((wide_slots < time_count - lag)[:, None, None], near[None], far[None])
        product = jnp.einsum("uik,ukl->uil", left, window, preferred_element_type=jnp.float32)
        backward = backward + jnp.where(
            (slots < time_count - lag)[:, None, None],
            product[:time_count],
            jnp.zeros((), jnp.float32),
        )
        forward = forward + jnp.where(
            (slots >= time_count - lag - 1)[:, None, None], product[1:], jnp.zeros((), jnp.float32)
        )
        return (forward, backward)

    empty_rows = jnp.zeros((time_count, rows_each, states), jnp.float32)
    forward, backward = lax.fori_loop(0, time_count // 2, pair_step, (empty_rows, empty_rows))
    convolved = step_size * (forward + backward[::-1])
    row_ids = first_row + jnp.arange(rows_each, dtype=jnp.int32)
    row_rates = lax.dynamic_slice_in_dim(energies[0], first_row, rows_each, 0)
    decay_rows = jnp.exp(-step_size * row_rates)

    def advance(running, term):
        running = decay_rows[:, None] * running + term
        return (running, running)

    _, summed = lax.scan(advance, jnp.zeros((rows_each, states), jnp.float32), convolved)
    moments = jnp.arange(time_count).astype(jnp.float32) * step_size
    live_rows = row_ids < sector_sizes[0]
    free_part = jnp.where(
        live_rows[None, :],
        jnp.exp(-row_rates[None, :] * moments[:, None]),
        jnp.zeros((), jnp.float32),
    )
    diagonal = jnp.where(
        (row_ids[:, None] == positions[None, :])[None],
        free_part[:, :, None],
        jnp.zeros((), jnp.float32),
    )
    new_rows = (diagonal - step_size * summed).astype(jnp.bfloat16)
    return lax.all_to_all(new_rows, "tm", split_axis=0, concat_axis=1, tiled=True)[None]


def solution(mesh):
    placed = (
        P("sector", "tm", None, None),
        P("sector", None, None),
        P("sector", None),
        P("tm"),
        P("tm"),
        P("sector"),
    )
    return jax.shard_map(
        per_device,
        mesh=mesh,
        in_specs=placed,
        out_specs=P("sector", "tm", None, None),
        check_vma=False,
    )
```

profile of v0, /device:TPU:32, one launch (start us, length us, event | category | flops | bytes accessed | tf_op | source)
XLA Modules:
  0.0 278.3 jit_solution(17964893264941335905)
XLA Ops:
  7.3 2.4 and_select_fusion.1
  9.7 1.9 collective-permute-start.1
  11.7 2.9 %fusion.15 = bf16[1,640,640]{2,1,0:T(8,128)(2,1)} fusion(bf16[1,1,640,640]{3,2,1,0:T(8,128)(2,1)S(1)} %copy-done.2, bf16[1,640,640]{2,1,0:T(8,128)(2,1)S(1)} %copy-done, pred[640]{0:T(1024)(128)(4,1)S(1)} %iota_compare_fusion.4), kind=kOutput, calls=%fused_computation.33 | convolution fusion | flops 1050214400 | bytes 2458240 | tf_op jit(solution)/shard_map/tik,jk->tij/dot_general | solution.py:54
  14.6 2.4 collective-permute-start
  18.3 3.6 %collective-permute-done.1 = bf16[1,640,640]{2,1,0:T(8,128)(2,1)S(1)} collective-permute-done((bf16[1,640,640]{2,1,0:T(8,128)(2,1)}, bf16[1,640,640]{2,1,0:T(8,128)(2,1)S(1)}, u32[]{:S(2)}, u32[]{:S(2)}) %collective-permute-start.1) | collective-permute-done | bytes 819232 | tf_op jit(solution)/shard_map/ppermute | solution.py:10
  21.8 6.6 %collective-permute-done = bf16[1,640,640]{2,1,0:T(8,128)(2,1)S(1)} collective-permute-done((bf16[1,640,640]{2,1,0:T(8,128)(2,1)}, bf16[1,640,640]{2,1,0:T(8,128)(2,1)S(1)}, u32[]{:S(2)}, u32[]{:S(2)}) %collective-permute-start) | collective-permute-done | bytes 819232 | tf_op jit(solution)/shard_map/ppermute | solution.py:10
  29.3 3.5 %fusion.13 = bf16[1,640,640]{2,1,0:T(8,128)(2,1)S(1)} fusion(bf16[1,640,640]{2,1,0:T(8,128)(2,1)} %copy-done.3, bf16[1,640,640]{2,1,0:T(8,128)(2,1)S(1)} %collective-permute-done.1, bf16[1,640,640]{2,1,0:T(8,128)(2,1)S(1)} %copy-done, f32[]{:T(128)} %bitcast.67, f32[]{:T(128)} %bitcast.66, pred[640]{0:T(1024)(128)(4,1)S(1)} %iota_compare_fusion.4), kind=kOutput, calls=%fused_computation.24 | convolution fusion | flops 1051852800 | bytes 3277448 | tf_op jit(solution)/shard_map/tik,kl->til/dot_general | solution.py:62
  33.5 7.0 %all-to-all-start = ((bf16[16,1,16,640]{3,2,1,0:T(8,128)(2,1)}), bf16[16,1,16,640]{3,2,1,0:T(8,128)(2,1)S(1)}, u32[]{:S(2)}, u32[]{:S(2)}) async-start(bf16[16,1,16,640]{3,2,1,0:T(8,128)(2,1)} %split.8), calls=%async_computation | async-start | bytes 655360 | tf_op jit(solution)/shard_map/all_to_all | solution.py:37
  42.2 7.4 %all-to-all-done = bf16[16,1,16,640]{3,2,1,0:T(8,128)(2,1)S(1)} async-done(((bf16[16,1,16,640]{3,2,1,0:T(8,128)(2,1)}), bf16[16,1,16,640]{3,2,1,0:T(8,128)(2,1)S(1)}, u32[]{:S(2)}, u32[]{:S(2)}) %all-to-all-start) | async-done | bytes 327712 | tf_op jit(solution)/shard_map/all_to_all | solution.py:37
  49.6 3.7 %all-to-all-start.1 = ((bf16[16,1,24,640]{3,2,1,0:T(8,128)(2,1)}), bf16[16,1,24,640]{3,2,1,0:T(8,128)(2,1)S(1)}, u32[]{:S(2)}, u32[]{:S(2)}) async-start(bf16[16,1,24,640]{3,2,1,0:T(8,128)(2,1)} %split.9), calls=%async_computation.1 | async-start | bytes 983040 | tf_op jit(solution)/shard_map/all_to_all | solution.py:37
  53.5 14.7 %all-to-all-done.1 = bf16[16,1,24,640]{3,2,1,0:T(8,128)(2,1)S(1)} async-done(((bf16[16,1,24,640]{3,2,1,0:T(8,128)(2,1)}), bf16[16,1,24,640]{3,2,1,0:T(8,128)(2,1)S(1)}, u32[]{:S(2)}, u32[]{:S(2)}) %all-to-all-start.1) | async-done | bytes 491552 | tf_op jit(solution)/shard_map/all_to_all | solution.py:37
  68.2 42.9 %all-gather.2.cloned.1.call-done = bf16[16,640,640]{2,1,0:T(8,128)(2,1)} async-done(((bf16[1,640,640]{2,1,0:T(8,128)(2,1)}), bf16[16,640,640]{2,1,0:T(8,128)(2,1)}) %all-gather.2.cloned.1.call-update) | async-done | bytes 13107216 | tf_op jit(solution)/shard_map/all_gather | solution.py:71
  111.1 10.8 %rev.6 = bf16[16,640,640]{2,1,0:T(8,128)(2,1)} reverse(bf16[16,640,640]{2,1,0:T(8,128)(2,1)} %all-gather.2.cloned.1.call-done), dimensions={0} | reverse | bytes 26214400 | tf_op jit(solution)/shard_map/rev | solution.py:72
  122.0 18.6 %pad_maximum_fusion = bf16[32,640,640]{2,1,0:T(8,128)(2,1)} fusion(bf16[16,640,640]{2,1,0:T(8,128)(2,1)} %all-gather.2.cloned.1.call-done, bf16[16,640,640]{2,1,0:T(8,128)(2,1)} %rev.6), kind=kLoop, calls=%fused_computation.21 | loop fusion | flops 13107200 | bytes 52428800 | tf_op jit(solution)/shard_map/concatenate | solution.py:72
  140.6 90.8 %while.35 = (s32[]{:T(128)}, f32[16,40,640]{2,1,0:T(8,128)}, f32[16,40,640]{2,1,0:T(8,128)}, bf16[16,40,640]{2,1,0:T(8,128)(2,1)S(1)}, bf16[32,640,640]{2,1,0:T(...) while((s32[]{:T(128)}, f32[16,40,640]{2,1,0:T(8,128)}, ...), condition=%wide.region_1.2_spmd.clone.clone, body=%wide.region_0.1_spmd.clone.clone.sunk | while | flops 559948800 | bytes 25805600 | solution.py:95
  140.6 7.3 %fusion.40 = f32[17,40,640]{2,1,0:T(8,128)S(1)} fusion(bf16[32,640,640]{2,1,0:T(8,128)(2,1)} %get-tuple-element.458, s32[]{:T(128)} %get-tuple-element.444, pred[17]{0:T(512)(128)(4,1)S(1)} %iota_compare_fusion.7, bf16[40,640]{1,0:T(8,128)(2,1)S(1)} %get-tuple-element.428, bf16[40,640]{1,0:T(8,128)(2,1)S(1)} %get-tuple-element.429), kind=kOutput, calls=%fused_computation.5.clone.1 | convolution fusion | flops 557491200 | bytes 15770129 | tf_op jit(solution)/shard_map/while/body/eval_jaxpr/uik,ukl->uil/dot_general | solution.py:83
  148.0 2.3 fusion.41
  150.3 7.3 %fusion.40 = f32[17,40,640]{2,1,0:T(8,128)S(1)} fusion(bf16[32,640,640]{2,1,0:T(8,128)(2,1)} %get-tuple-element.458, s32[]{:T(128)} %get-tuple-element.444, pred[17]{0:T(512)(128)(4,1)S(1)} %iota_compare_fusion.7, bf16[40,640]{1,0:T(8,128)(2,1)S(1)} %get-tuple-element.428, bf16[40,640]{1,0:T(8,128)(2,1)S(1)} %get-tuple-element.429), kind=kOutput, calls=%fused_computation.5.clone.1 | convolution fusion | flops 557491200 | bytes 15770129 | tf_op jit(solution)/shard_map/while/body/eval_jaxpr/uik,ukl->uil/dot_general | solution.py:83
  157.6 4.2 %fusion.41 = (f32[16,40,640]{2,1,0:T(8,128)}, f32[16,40,640]{2,1,0:T(8,128)}) fusion(f32[17,40,640]{2,1,0:T(8,128)S(1)} %fusion.40, f32[16,40,640]{2,1,0:T(8,128)} %get-tuple-element.446, pred[16]{0:T(512)(128)(4,1)S(1)} %get-tuple-element.430, pred[]{:T(512)S(6)} %compare.7, pred[16]{0:T(512)(128)(4,1)S(1)} %get-tuple-element.431, ...), kind=kLoop, calls=%fused_computation.8.clone.1 | loop fusion | flops 2457600 | bytes 9830433 | tf_op jit(solution)/shard_map/while/body/eval_jaxpr/add | solution.py:84
  161.9 7.3 %fusion.40 = f32[17,40,640]{2,1,0:T(8,128)S(1)} fusion(bf16[32,640,640]{2,1,0:T(8,128)(2,1)} %get-tuple-element.458, s32[]{:T(128)} %get-tuple-element.444, pred[17]{0:T(512)(128)(4,1)S(1)} %iota_compare_fusion.7, bf16[40,640]{1,0:T(8,128)(2,1)S(1)} %get-tuple-element.428, bf16[40,640]{1,0:T(8,128)(2,1)S(1)} %get-tuple-element.429), kind=kOutput, calls=%fused_computation.5.clone.1 | convolution fusion | flops 557491200 | bytes 15770129 | tf_op jit(solution)/shard_map/while/body/eval_jaxpr/uik,ukl->uil/dot_general | solution.py:83
  169.2 4.2 %fusion.41 = (f32[16,40,640]{2,1,0:T(8,128)}, f32[16,40,640]{2,1,0:T(8,128)}) fusion(f32[17,40,640]{2,1,0:T(8,128)S(1)} %fusion.40, f32[16,40,640]{2,1,0:T(8,128)} %get-tuple-element.446, pred[16]{0:T(512)(128)(4,1)S(1)} %get-tuple-element.430, pred[]{:T(512)S(6)} %compare.7, pred[16]{0:T(512)(128)(4,1)S(1)} %get-tuple-element.431, ...), kind=kLoop, calls=%fused_computation.8.clone.1 | loop fusion | flops 2457600 | bytes 9830433 | tf_op jit(solution)/shard_map/while/body/eval_jaxpr/add | solution.py:84
  173.5 7.3 %fusion.40 = f32[17,40,640]{2,1,0:T(8,128)S(1)} fusion(bf16[32,640,640]{2,1,0:T(8,128)(2,1)} %get-tuple-element.458, s32[]{:T(128)} %get-tuple-element.444, pred[17]{0:T(512)(128)(4,1)S(1)} %iota_compare_fusion.7, bf16[40,640]{1,0:T(8,128)(2,1)S(1)} %get-tuple-element.428, bf16[40,640]{1,0:T(8,128)(2,1)S(1)} %get-tuple-element.429), kind=kOutput, calls=%fused_computation.5.clone.1 | convolution fusion | flops 557491200 | bytes 15770129 | tf_op jit(solution)/shard_map/while/body/eval_jaxpr/uik,ukl->uil/dot_general | solution.py:83
  180.8 4.2 %fusion.41 = (f32[16,40,640]{2,1,0:T(8,128)}, f32[16,40,640]{2,1,0:T(8,128)}) fusion(f32[17,40,640]{2,1,0:T(8,128)S(1)} %fusion.40, f32[16,40,640]{2,1,0:T(8,128)} %get-tuple-element.446, pred[16]{0:T(512)(128)(4,1)S(1)} %get-tuple-element.430, pred[]{:T(512)S(6)} %compare.7, pred[16]{0:T(512)(128)(4,1)S(1)} %get-tuple-element.431, ...), kind=kLoop, calls=%fused_computation.8.clone.1 | loop fusion | flops 2457600 | bytes 9830433 | tf_op jit(solution)/shard_map/while/body/eval_jaxpr/add | solution.py:84
  185.1 7.3 %fusion.40 = f32[17,40,640]{2,1,0:T(8,128)S(1)} fusion(bf16[32,640,640]{2,1,0:T(8,128)(2,1)} %get-tuple-element.458, s32[]{:T(128)} %get-tuple-element.444, pred[17]{0:T(512)(128)(4,1)S(1)} %iota_compare_fusion.7, bf16[40,640]{1,0:T(8,128)(2,1)S(1)} %get-tuple-element.428, bf16[40,640]{1,0:T(8,128)(2,1)S(1)} %get-tuple-element.429), kind=kOutput, calls=%fused_computation.5.clone.1 | convolution fusion | flops 557491200 | bytes 15770129 | tf_op jit(solution)/shard_map/while/body/eval_jaxpr/uik,ukl->uil/dot_general | solution.py:83
  192.4 4.2 %fusion.41 = (f32[16,40,640]{2,1,0:T(8,128)}, f32[16,40,640]{2,1,0:T(8,128)}) fusion(f32[17,40,640]{2,1,0:T(8,128)S(1)} %fusion.40, f32[16,40,640]{2,1,0:T(8,128)} %get-tuple-element.446, pred[16]{0:T(512)(128)(4,1)S(1)} %get-tuple-element.430, pred[]{:T(512)S(6)} %compare.7, pred[16]{0:T(512)(128)(4,1)S(1)} %get-tuple-element.431, ...), kind=kLoop, calls=%fused_computation.8.clone.1 | loop fusion | flops 2457600 | bytes 9830433 | tf_op jit(solution)/shard_map/while/body/eval_jaxpr/add | solution.py:84
  196.7 7.3 %fusion.40 = f32[17,40,640]{2,1,0:T(8,128)S(1)} fusion(bf16[32,640,640]{2,1,0:T(8,128)(2,1)} %get-tuple-element.458, s32[]{:T(128)} %get-tuple-element.444, pred[17]{0:T(512)(128)(4,1)S(1)} %iota_compare_fusion.7, bf16[40,640]{1,0:T(8,128)(2,1)S(1)} %get-tuple-element.428, bf16[40,640]{1,0:T(8,128)(2,1)S(1)} %get-tuple-element.429), kind=kOutput, calls=%fused_computation.5.clone.1 | convolution fusion | flops 557491200 | bytes 15770129 | tf_op jit(solution)/shard_map/while/body/eval_jaxpr/uik,ukl->uil/dot_general | solution.py:83
  204.0 4.2 %fusion.41 = (f32[16,40,640]{2,1,0:T(8,128)}, f32[16,40,640]{2,1,0:T(8,128)}) fusion(f32[17,40,640]{2,1,0:T(8,128)S(1)} %fusion.40, f32[16,40,640]{2,1,0:T(8,128)} %get-tuple-element.446, pred[16]{0:T(512)(128)(4,1)S(1)} %get-tuple-element.430, pred[]{:T(512)S(6)} %compare.7, pred[16]{0:T(512)(128)(4,1)S(1)} %get-tuple-element.431, ...), kind=kLoop, calls=%fused_computation.8.clone.1 | loop fusion | flops 2457600 | bytes 9830433 | tf_op jit(solution)/shard_map/while/body/eval_jaxpr/add | solution.py:84
  208.2 7.3 %fusion.40 = f32[17,40,640]{2,1,0:T(8,128)S(1)} fusion(bf16[32,640,640]{2,1,0:T(8,128)(2,1)} %get-tuple-element.458, s32[]{:T(128)} %get-tuple-element.444, pred[17]{0:T(512)(128)(4,1)S(1)} %iota_compare_fusion.7, bf16[40,640]{1,0:T(8,128)(2,1)S(1)} %get-tuple-element.428, bf16[40,640]{1,0:T(8,128)(2,1)S(1)} %get-tuple-element.429), kind=kOutput, calls=%fused_computation.5.clone.1 | convolution fusion | flops 557491200 | bytes 15770129 | tf_op jit(solution)/shard_map/while/body/eval_jaxpr/uik,ukl->uil/dot_general | solution.py:83
  215.6 4.2 %fusion.41 = (f32[16,40,640]{2,1,0:T(8,128)}, f32[16,40,640]{2,1,0:T(8,128)}) fusion(f32[17,40,640]{2,1,0:T(8,128)S(1)} %fusion.40, f32[16,40,640]{2,1,0:T(8,128)} %get-tuple-element.446, pred[16]{0:T(512)(128)(4,1)S(1)} %get-tuple-element.430, pred[]{:T(512)S(6)} %compare.7, pred[16]{0:T(512)(128)(4,1)S(1)} %get-tuple-element.431, ...), kind=kLoop, calls=%fused_computation.8.clone.1 | loop fusion | flops 2457600 | bytes 9830433 | tf_op jit(solution)/shard_map/while/body/eval_jaxpr/add | solution.py:84
  219.8 7.3 %fusion.40 = f32[17,40,640]{2,1,0:T(8,128)S(1)} fusion(bf16[32,640,640]{2,1,0:T(8,128)(2,1)} %get-tuple-element.458, s32[]{:T(128)} %get-tuple-element.444, pred[17]{0:T(512)(128)(4,1)S(1)} %iota_compare_fusion.7, bf16[40,640]{1,0:T(8,128)(2,1)S(1)} %get-tuple-element.428, bf16[40,640]{1,0:T(8,128)(2,1)S(1)} %get-tuple-element.429), kind=kOutput, calls=%fused_computation.5.clone.1 | convolution fusion | flops 557491200 | bytes 15770129 | tf_op jit(solution)/shard_map/while/body/eval_jaxpr/uik,ukl->uil/dot_general | solution.py:83
  227.1 4.2 %fusion.41 = (f32[16,40,640]{2,1,0:T(8,128)}, f32[16,40,640]{2,1,0:T(8,128)}) fusion(f32[17,40,640]{2,1,0:T(8,128)S(1)} %fusion.40, f32[16,40,640]{2,1,0:T(8,128)} %get-tuple-element.446, pred[16]{0:T(512)(128)(4,1)S(1)} %get-tuple-element.430, pred[]{:T(512)S(6)} %compare.7, pred[16]{0:T(512)(128)(4,1)S(1)} %get-tuple-element.431, ...), kind=kLoop, calls=%fused_computation.8.clone.1 | loop fusion | flops 2457600 | bytes 9830433 | tf_op jit(solution)/shard_map/while/body/eval_jaxpr/add | solution.py:84
  231.4 3.3 %add_multiply_fusion = f32[16,40,640]{2,1,0:T(8,128)} fusion(f32[16,40,640]{2,1,0:T(8,128)} %get-tuple-element.265, f32[16,40,640]{2,1,0:T(8,128)} %get-tuple-element.266), kind=kLoop, calls=%fused_computation.27 | loop fusion | flops 819200 | bytes 4915200 | tf_op jit(solution)/shard_map/mul | solution.py:96
  234.7 16.0 %while.34 = (s32[]{:T(128)}, f32[40,640]{1,0:T(8,128)S(1)}, f32[16,40,640]{2,1,0:T(8,128)S(1)}, f32[40]{0:T(128)S(1)}, f32[16,40,640]{2,1,0:T(8,128)}, /*index=5*/s32[]{:T(128)}, s32[]{:T(128)}) while((s32[]{:T(128)}, f32[40,640]{1,0:T(8,128)S(1)}, f32[16,40,640]{2,1,0:T(8,128)S(1)}, f32[40]{0:T(128)S(1)}, ...), condition=%wide.region_3.4_spmd.clone, body=%wide.region_2.3_spmd.clone.sunk | while | flops 76803 | bytes 410203 | solution.py:105
  234.8 1.0 bitcast_dynamic-update-slice_fusion.2
  235.8 1.0 bitcast_dynamic-update-slice_fusion.2
  237.8 1.0 bitcast_dynamic-update-slice_fusion.2
  238.8 1.0 bitcast_dynamic-update-slice_fusion.2
  239.8 1.0 bitcast_dynamic-update-slice_fusion.2
  240.8 1.0 bitcast_dynamic-update-slice_fusion.2
  241.8 1.0 bitcast_dynamic-update-slice_fusion.2
  242.8 1.0 bitcast_dynamic-update-slice_fusion.2
  243.8 1.0 bitcast_dynamic-update-slice_fusion.2
  244.8 1.0 bitcast_dynamic-update-slice_fusion.2
  245.8 1.0 bitcast_dynamic-update-slice_fusion.2
  246.8 1.0 bitcast_dynamic-update-slice_fusion.2
  247.8 1.0 bitcast_dynamic-update-slice_fusion.2
  249.8 1.0 bitcast_dynamic-update-slice_fusion.2
  251.1 19.5 %all_to_all.19 = bf16[16,40,640]{2,1,0:T(8,128)(2,1)S(1)} all-to-all(bf16[16,40,640]{2,1,0:T(8,128)(2,1)S(1)} %subtract_convert_fusion), channel_id=1, replica_groups=mesh['tm'=16,'sector'=8] {'tm'}, dimensions={0} | all-to-all | bytes 1638400 | tf_op jit(solution)/shard_map/all_to_all | solution.py:119
  (52 shorter events, 7.0 us)
Async XLA Ops:
  6.5 5.1 %copy-start = (bf16[1,640,640]{2,1,0:T(8,128)(2,1)S(1)}, bf16[1,640,640]{2,1,0:T(8,128)(2,1)}, u32[]{:S(2)}) copy-start(bf16[1,640,640]{2,1,0:T(8,128)(2,1)} %param.11) | copy-start | bytes 2457604
  6.5 5.1 %copy-start.2 = (bf16[1,1,640,640]{3,2,1,0:T(8,128)(2,1)S(1)}, bf16[1,1,640,640]{3,2,1,0:T(8,128)(2,1)}, u32[]{:S(2)}) copy-start(bf16[1,1,640,640]{3,2,1,0:T(8,128)(2,1)} %param.10) | copy-start | bytes 2457604
  6.5 104.6 %all-gather.2.cloned.1.call-start = ((), (), s32[]{:S(2)}) async-start(), calls=%async_computation.3 | async-start | bytes 13926400 | tf_op jit(solution)/shard_map/all_gather | solution.py:71
  9.7 12.1 %collective-permute-start.1 = (bf16[1,640,640]{2,1,0:T(8,128)(2,1)}, bf16[1,640,640]{2,1,0:T(8,128)(2,1)S(1)}, u32[]{:S(2)}, u32[]{:S(2)}) collective-permute-start(bf16[1,640,640]{2,1,0:T(8,128)(2,1)} %and_select_fusion.1), channel_id=1, source_target_pairs={{1,0},{2,1},{3,2},{4,3},{5,4},{6,5},{7,6},{9,8},{10,9},{11,10},{12... | collective-permute-start | bytes 2457608 | tf_op jit(solution)/shard_map/ppermute | solution.py:10
  14.6 13.9 %collective-permute-start = (bf16[1,640,640]{2,1,0:T(8,128)(2,1)}, bf16[1,640,640]{2,1,0:T(8,128)(2,1)S(1)}, u32[]{:S(2)}, u32[]{:S(2)}) collective-permute-start(bf16[1,640,640]{2,1,0:T(8,128)(2,1)} %fusion.15), channel_id=1, source_target_pairs={{0,1},{1,2},{2,3},{3,4},{4,5},{5,6},{6,7},{8,9},{9,10},{10,11},{11... | collective-permute-start | bytes 2457608 | tf_op jit(solution)/shard_map/ppermute | solution.py:10
  28.4 0.9 copy-start.3
  33.5 16.0 %all-to-all-start = ((bf16[16,1,16,640]{3,2,1,0:T(8,128)(2,1)}), bf16[16,1,16,640]{3,2,1,0:T(8,128)(2,1)S(1)}, u32[]{:S(2)}, u32[]{:S(2)}) async-start(bf16[16,1,16,640]{3,2,1,0:T(8,128)(2,1)} %split.8), calls=%async_computation | async-start | bytes 655360 | tf_op jit(solution)/shard_map/all_to_all | solution.py:37
  49.6 18.6 %all-to-all-start.1 = ((bf16[16,1,24,640]{3,2,1,0:T(8,128)(2,1)}), bf16[16,1,24,640]{3,2,1,0:T(8,128)(2,1)S(1)}, u32[]{:S(2)}, u32[]{:S(2)}) async-start(bf16[16,1,24,640]{3,2,1,0:T(8,128)(2,1)} %split.9), calls=%async_computation.1 | async-start | bytes 983040 | tf_op jit(solution)/shard_map/all_to_all | solution.py:37
  250.8 20.7 %copy-start.1 = (bf16[1,640,640]{2,1,0:T(8,128)(2,1)S(1)}, bf16[1,640,640]{2,1,0:T(8,128)(2,1)}, u32[]{:S(2)}) copy-start(bf16[1,640,640]{2,1,0:T(8,128)(2,1)} %param.11) | copy-start | bytes 2457604
Sparse Core Ops, SparseCore 0:
  9.8 101.2 all-gather.1
where the time goes:
time: 280 us; the launch traced here: 278 us
  waiting for transfers between devices  75.2 us (27%)
  other arithmetic  73.3 us (26%)
  matrix products  64.8 us (23%)
  blocking collectives  19.5 us (7%)
  between operations  15.6 us (6%)
  starting transfers between devices  15 us (5%)
  local copies, waits for them, and re-layouts  14.4 us (5%)
    dot_general x8, matrix products, pair_step(): jnp.einsum('uik,ukl->uil', left, window, preferred_element_type=jnp.float32)  58.4 us
    all_gather x1, waiting for transfers between devices, per_device(): history = lax.all_gather(masked_prop, 'tm', axis=0, tiled=True)  42.9 us
    add x8, other arithmetic, pair_step(): backward + jnp.where((slots < time_count - lag)[:, None, None], product[:...  31.9 us
    all_to_all x2, waiting for transfers between devices, several_exchanges(): lax.all_to_all(share, axis, split_axis=0, concat_axis=0, tiled=True)  22 us
    all_to_all x1, blocking collectives, per_device(): lax.all_to_all(new_rows, 'tm', split_axis=0, concat_axis=1, tiled=True)  19.5 us
    concatenate x1, other arithmetic, per_device(): mirrored = jnp.concatenate([history[::-1], history], 0)  18.6 us
    dynamic_update_slice x16, other arithmetic, per_device(): lax.scan(advance, jnp.zeros((rows_each, states), jnp.float32), convolved)  15.7 us
    rev x1, local copies, waits for them, and re-layouts, per_device(): mirrored = jnp.concatenate([history[::-1], history], 0)  10.8 us
  transfers between devices with their start and end apart: 5, of which 5 were waited for; matrix products, arithmetic and copies ran while one was open for 3% of the time, Pallas kernels for 0%

commit v1 on v0

--- a/solution.py
+++ b/solution.py
@@ -68,7 +68,12 @@
     rows_each = states // lax.axis_size("tm")
     first_row = lax.axis_index("tm") * rows_each
     lag_rows = several_exchanges(self_energy, "tm", 2, 1, 0)
-    history = lax.all_gather(masked_prop, "tm", axis=0, tiled=True)
+    history = jnp.concatenate(
+        jax.lax.all_to_all(
+            jnp.stack(tuple((masked_prop for _ in range(jax.lax.axis_size("tm"))))), "tm", 0, 0
+        ),
+        0,
+    )
     mirrored = jnp.concatenate([history[::-1], history], 0)
     slots = jnp.arange(time_count, dtype=jnp.int32)
     wide_slots = jnp.arange(time_count + 1, dtype=jnp.int32)

time: 280 us -> 462 us (1.65)
  waiting for transfers between devices: 75.2 us -> 244 us
  blocking collectives: 19.5 us -> 37.2 us
  between operations: 15.6 us -> 2.22 us
    all_to_all x0 -> x1, waiting for transfers between devices: none -> 227 us  [per_device(): jax.lax.all_to_all(jnp.stack(tuple((masked_prop for _ in range(jax.lax.ax...]
    all_gather x1 -> x0, waiting for transfers between devices: 42.9 us -> none  [per_device(): history = lax.all_gather(masked_prop, 'tm', axis=0, tiled=True)]
    all_to_all x0 -> x1, blocking collectives: none -> 16 us  [several_exchanges(): lax.all_to_all(share, axis, split_axis=0, concat_axis=0, tiled=True)]
    all_to_all x2 -> x1, waiting for transfers between devices: 22 us -> 9.09 us  [several_exchanges(): lax.all_to_all(share, axis, split_axis=0, concat_axis=0, tiled=True)]
    another operation x0 -> x1, local copies, waits for them, and re-layouts: none -> 6.23 us  [per_device(): jnp.stack(tuple((masked_prop for _ in range(jax.lax.axis_size('tm')))))]
    all_to_all x0 -> x1, starting transfers between devices: none -> 4.95 us  [per_device(): jax.lax.all_to_all(jnp.stack(tuple((masked_prop for _ in range(jax.lax.ax...]
    all_to_all x2 -> x1, starting transfers between devices: 10.7 us -> 7.03 us  [several_exchanges(): lax.all_to_all(share, axis, split_axis=0, concat_axis=0, tiled=True)]
  transfers between devices with their start and end apart: 5 -> 4, of which waited for: 5 -> 4; matrix products, arithmetic and copies ran while one was open for 3% -> 0% of each run, Pallas kernels for 0% -> 0%
where the time goes in v1:
time: 462 us; the launch traced here: 458 us
  waiting for transfers between devices  244 us (53%)
  other arithmetic  72.7 us (16%)
  matrix products  64.7 us (14%)
  blocking collectives  37.2 us (8%)
  local copies, waits for them, and re-layouts  19 us (4%)
  starting transfers between devices  17.5 us (4%)
    all_to_all x1, waiting for transfers between devices, per_device(): jax.lax.all_to_all(jnp.stack(tuple((masked_prop for _ in range(jax.lax.ax...  227 us
    dot_general x8, matrix products, pair_step(): jnp.einsum('uik,ukl->uil', left, window, preferred_element_type=jnp.float32)  58.4 us
    add x8, other arithmetic, pair_step(): backward + jnp.where((slots < time_count - lag)[:, None, None], product[:...  31.9 us
    all_to_all x1, blocking collectives, per_device(): lax.all_to_all(new_rows, 'tm', split_axis=0, concat_axis=1, tiled=True)  21.2 us
    concatenate x1, other arithmetic, per_device(): mirrored = jnp.concatenate([history[::-1], history], 0)  18.6 us
    all_to_all x1, blocking collectives, several_exchanges(): lax.all_to_all(share, axis, split_axis=0, concat_axis=0, tiled=True)  16 us
    dynamic_update_slice x16, other arithmetic, per_device(): lax.scan(advance, jnp.zeros((rows_each, states), jnp.float32), convolved)  15.7 us
    rev x1, local copies, waits for them, and re-layouts, per_device(): mirrored = jnp.concatenate([history[::-1], history], 0)  10.8 us
  transfers between devices with their start and end apart: 4, of which 4 were waited for; matrix products, arithmetic and copies ran while one was open for 0% of the time, Pallas kernels for 0%

profile of v1, /device:TPU:32, one launch (start us, length us, event | category | flops | bytes accessed | tf_op | source)
XLA Modules:
  0.0 458.1 jit_solution(13823455452847331370)
XLA Ops:
  0.7 1.5 fusion.17
  2.2 2.8 fusion.15
  5.0 1.9 collective-permute-start
  7.2 3.6 collective-permute-start.1
  12.2 6.7 %collective-permute-done = bf16[1,640,640]{2,1,0:T(8,128)(2,1)S(1)} collective-permute-done((bf16[1,640,640]{2,1,0:T(8,128)(2,1)}, bf16[1,640,640]{2,1,0:T(8,128)(2,1)S(1)}, u32[]{:S(2)}, u32[]{:S(2)}) %collective-permute-start) | collective-permute-done | bytes 819232 | tf_op jit(solution)/shard_map/ppermute | solution.py:10
  18.9 1.9 collective-permute-done.1
  20.7 3.5 fusion.13
  25.0 7.0 %all-to-all-start = ((bf16[16,1,16,640]{3,2,1,0:T(8,128)(2,1)}), bf16[16,1,16,640]{3,2,1,0:T(8,128)(2,1)S(1)}, u32[]{:S(2)}, u32[]{:S(2)}) async-start(bf16[16,1,16,640]{3,2,1,0:T(8,128)(2,1)} %split.8), calls=%async_computation | async-start | bytes 655360 | tf_op jit(solution)/shard_map/all_to_all | solution.py:37
  32.0 9.1 %all-to-all-done = bf16[16,1,16,640]{3,2,1,0:T(8,128)(2,1)S(1)} async-done(((bf16[16,1,16,640]{3,2,1,0:T(8,128)(2,1)}), bf16[16,1,16,640]{3,2,1,0:T(8,128)(2,1)S(1)}, u32[]{:S(2)}, u32[]{:S(2)}) %all-to-all-start) | async-done | bytes 327712 | tf_op jit(solution)/shard_map/all_to_all | solution.py:37
  41.1 16.0 %all_to_all.24 = bf16[16,1,24,640]{3,2,1,0:T(8,128)(2,1)S(1)} all-to-all(bf16[16,1,24,640]{3,2,1,0:T(8,128)(2,1)S(1)} %split.9), channel_id=1, replica_groups=mesh['tm'=16,'sector'=8] {'tm'}, dimensions={0} | all-to-all | bytes 983040 | tf_op jit(solution)/shard_map/all_to_all | solution.py:37
  57.2 6.2 %stack.5 = bf16[16,1,640,640]{3,2,1,0:T(8,128)(2,1)} broadcast(bf16[640,640]{1,0:T(8,128)(2,1)S(1)} %fusion.17), dimensions={2,3} | broadcast | bytes 13926400 | tf_op jit(solution)/shard_map/stack | solution.py:73
  63.4 5.0 %all-to-all-start.2 = ((bf16[16,1,640,640]{3,2,1,0:T(8,128)(2,1)}), bf16[16,1,640,640]{3,2,1,0:T(8,128)(2,1)}, u32[]{:S(2)}, u32[]{:S(2)}) async-start(bf16[16,1,640,640]{3,2,1,0:T(8,128)(2,1)} %stack.5), calls=%async_computation.2 | async-start | bytes 26214400 | tf_op jit(solution)/shard_map/all_to_all | solution.py:72
  69.4 226.7 %all-to-all-done.2 = bf16[16,1,640,640]{3,2,1,0:T(8,128)(2,1)} async-done(((bf16[16,1,640,640]{3,2,1,0:T(8,128)(2,1)}), bf16[16,1,640,640]{3,2,1,0:T(8,128)(2,1)}, u32[]{:S(2)}, u32[]{:S(2)}) %all-to-all-start.2) | async-done | bytes 13107232 | tf_op jit(solution)/shard_map/all_to_all | solution.py:72
  296.1 10.8 %rev.6 = bf16[16,640,640]{2,1,0:T(8,128)(2,1)} reverse(bf16[16,640,640]{2,1,0:T(8,128)(2,1)} %bitcast.21), dimensions={0} | reverse | bytes 26214400 | tf_op jit(solution)/shard_map/rev | solution.py:77
  306.9 18.6 %pad_maximum_fusion = bf16[32,640,640]{2,1,0:T(8,128)(2,1)} fusion(bf16[16,640,640]{2,1,0:T(8,128)(2,1)} %bitcast.21, bf16[16,640,640]{2,1,0:T(8,128)(2,1)} %rev.6), kind=kLoop, calls=%fused_computation.21 | loop fusion | flops 13107200 | bytes 52428800 | tf_op jit(solution)/shard_map/concatenate | solution.py:77
  325.5 90.8 %while.35 = (s32[]{:T(128)}, f32[16,40,640]{2,1,0:T(8,128)}, f32[16,40,640]{2,1,0:T(8,128)}, bf16[16,40,640]{2,1,0:T(8,128)(2,1)S(1)}, bf16[32,640,640]{2,1,0:T(...) while((s32[]{:T(128)}, f32[16,40,640]{2,1,0:T(8,128)}, ...), condition=%wide.region_1.2_spmd.clone.clone, body=%wide.region_0.1_spmd.clone.clone.sunk | while | flops 559948800 | bytes 25805600 | solution.py:100
  325.6 7.3 %fusion.31 = f32[17,40,640]{2,1,0:T(8,128)S(1)} fusion(bf16[32,640,640]{2,1,0:T(8,128)(2,1)} %get-tuple-element.458, s32[]{:T(128)} %get-tuple-element.444, pred[17]{0:T(512)(128)(4,1)S(1)} %iota_compare_fusion.7, bf16[40,640]{1,0:T(8,128)(2,1)S(1)} %get-tuple-element.428, bf16[40,640]{1,0:T(8,128)(2,1)S(1)} %get-tuple-element.429), kind=kOutput, calls=%fused_computation.5.clone.1 | convolution fusion | flops 557491200 | bytes 15770129 | tf_op jit(solution)/shard_map/while/body/eval_jaxpr/uik,ukl->uil/dot_general | solution.py:88
  332.9 2.3 fusion.32
  335.2 7.3 %fusion.31 = f32[17,40,640]{2,1,0:T(8,128)S(1)} fusion(bf16[32,640,640]{2,1,0:T(8,128)(2,1)} %get-tuple-element.458, s32[]{:T(128)} %get-tuple-element.444, pred[17]{0:T(512)(128)(4,1)S(1)} %iota_compare_fusion.7, bf16[40,640]{1,0:T(8,128)(2,1)S(1)} %get-tuple-element.428, bf16[40,640]{1,0:T(8,128)(2,1)S(1)} %get-tuple-element.429), kind=kOutput, calls=%fused_computation.5.clone.1 | convolution fusion | flops 557491200 | bytes 15770129 | tf_op jit(solution)/shard_map/while/body/eval_jaxpr/uik,ukl->uil/dot_general | solution.py:88
  342.6 4.2 fusion.32
  346.8 7.3 %fusion.31 = f32[17,40,640]{2,1,0:T(8,128)S(1)} fusion(bf16[32,640,640]{2,1,0:T(8,128)(2,1)} %get-tuple-element.458, s32[]{:T(128)} %get-tuple-element.444, pred[17]{0:T(512)(128)(4,1)S(1)} %iota_compare_fusion.7, bf16[40,640]{1,0:T(8,128)(2,1)S(1)} %get-tuple-element.428, bf16[40,640]{1,0:T(8,128)(2,1)S(1)} %get-tuple-element.429), kind=kOutput, calls=%fused_computation.5.clone.1 | convolution fusion | flops 557491200 | bytes 15770129 | tf_op jit(solution)/shard_map/while/body/eval_jaxpr/uik,ukl->uil/dot_general | solution.py:88
  354.1 4.2 fusion.32
  358.4 7.3 %fusion.31 = f32[17,40,640]{2,1,0:T(8,128)S(1)} fusion(bf16[32,640,640]{2,1,0:T(8,128)(2,1)} %get-tuple-element.458, s32[]{:T(128)} %get-tuple-element.444, pred[17]{0:T(512)(128)(4,1)S(1)} %iota_compare_fusion.7, bf16[40,640]{1,0:T(8,128)(2,1)S(1)} %get-tuple-element.428, bf16[40,640]{1,0:T(8,128)(2,1)S(1)} %get-tuple-element.429), kind=kOutput, calls=%fused_computation.5.clone.1 | convolution fusion | flops 557491200 | bytes 15770129 | tf_op jit(solution)/shard_map/while/body/eval_jaxpr/uik,ukl->uil/dot_general | solution.py:88
  365.7 4.2 fusion.32
  370.0 7.3 %fusion.31 = f32[17,40,640]{2,1,0:T(8,128)S(1)} fusion(bf16[32,640,640]{2,1,0:T(8,128)(2,1)} %get-tuple-element.458, s32[]{:T(128)} %get-tuple-element.444, pred[17]{0:T(512)(128)(4,1)S(1)} %iota_compare_fusion.7, bf16[40,640]{1,0:T(8,128)(2,1)S(1)} %get-tuple-element.428, bf16[40,640]{1,0:T(8,128)(2,1)S(1)} %get-tuple-element.429), kind=kOutput, calls=%fused_computation.5.clone.1 | convolution fusion | flops 557491200 | bytes 15770129 | tf_op jit(solution)/shard_map/while/body/eval_jaxpr/uik,ukl->uil/dot_general | solution.py:88
  377.3 4.2 fusion.32
  381.6 7.3 %fusion.31 = f32[17,40,640]{2,1,0:T(8,128)S(1)} fusion(bf16[32,640,640]{2,1,0:T(8,128)(2,1)} %get-tuple-element.458, s32[]{:T(128)} %get-tuple-element.444, pred[17]{0:T(512)(128)(4,1)S(1)} %iota_compare_fusion.7, bf16[40,640]{1,0:T(8,128)(2,1)S(1)} %get-tuple-element.428, bf16[40,640]{1,0:T(8,128)(2,1)S(1)} %get-tuple-element.429), kind=kOutput, calls=%fused_computation.5.clone.1 | convolution fusion | flops 557491200 | bytes 15770129 | tf_op jit(solution)/shard_map/while/body/eval_jaxpr/uik,ukl->uil/dot_general | solution.py:88
  388.9 4.2 fusion.32
  393.1 7.3 %fusion.31 = f32[17,40,640]{2,1,0:T(8,128)S(1)} fusion(bf16[32,640,640]{2,1,0:T(8,128)(2,1)} %get-tuple-element.458, s32[]{:T(128)} %get-tuple-element.444, pred[17]{0:T(512)(128)(4,1)S(1)} %iota_compare_fusion.7, bf16[40,640]{1,0:T(8,128)(2,1)S(1)} %get-tuple-element.428, bf16[40,640]{1,0:T(8,128)(2,1)S(1)} %get-tuple-element.429), kind=kOutput, calls=%fused_computation.5.clone.1 | convolution fusion | flops 557491200 | bytes 15770129 | tf_op jit(solution)/shard_map/while/body/eval_jaxpr/uik,ukl->uil/dot_general | solution.py:88
  400.5 4.2 fusion.32
  404.7 7.3 %fusion.31 = f32[17,40,640]{2,1,0:T(8,128)S(1)} fusion(bf16[32,640,640]{2,1,0:T(8,128)(2,1)} %get-tuple-element.458, s32[]{:T(128)} %get-tuple-element.444, pred[17]{0:T(512)(128)(4,1)S(1)} %iota_compare_fusion.7, bf16[40,640]{1,0:T(8,128)(2,1)S(1)} %get-tuple-element.428, bf16[40,640]{1,0:T(8,128)(2,1)S(1)} %get-tuple-element.429), kind=kOutput, calls=%fused_computation.5.clone.1 | convolution fusion | flops 557491200 | bytes 15770129 | tf_op jit(solution)/shard_map/while/body/eval_jaxpr/uik,ukl->uil/dot_general | solution.py:88
  412.0 4.2 fusion.32
  416.3 3.3 add_multiply_fusion
  419.7 16.0 %while.34 = (s32[]{:T(128)}, f32[40,640]{1,0:T(8,128)S(1)}, f32[16,40,640]{2,1,0:T(8,128)S(1)}, f32[40]{0:T(128)S(1)}, f32[16,40,640]{2,1,0:T(8,128)}, /*index=5*/s32[]{:T(128)}, s32[]{:T(128)}) while((s32[]{:T(128)}, f32[40,640]{1,0:T(8,128)S(1)}, f32[16,40,640]{2,1,0:T(8,128)S(1)}, f32[40]{0:T(128)S(1)}, ...), condition=%wide.region_3.4_spmd.clone, body=%wide.region_2.3_spmd.clone.sunk | while | flops 76803 | bytes 410203 | solution.py:110
  419.7 1.0 bitcast_dynamic-update-slice_fusion.2
  420.7 1.0 bitcast_dynamic-update-slice_fusion.2
  422.7 1.0 bitcast_dynamic-update-slice_fusion.2
  423.7 1.0 bitcast_dynamic-update-slice_fusion.2
  424.7 1.0 bitcast_dynamic-update-slice_fusion.2
  425.7 1.0 bitcast_dynamic-update-slice_fusion.2
  426.7 1.0 bitcast_dynamic-update-slice_fusion.2
  427.7 1.0 bitcast_dynamic-update-slice_fusion.2
  428.7 1.0 bitcast_dynamic-update-slice_fusion.2
  429.7 1.0 bitcast_dynamic-update-slice_fusion.2
  430.7 1.0 bitcast_dynamic-update-slice_fusion.2
  431.7 1.0 bitcast_dynamic-update-slice_fusion.2
  432.7 1.0 bitcast_dynamic-update-slice_fusion.2
  436.0 21.2 %all_to_all.25 = bf16[16,40,640]{2,1,0:T(8,128)(2,1)S(1)} all-to-all(bf16[16,40,640]{2,1,0:T(8,128)(2,1)S(1)} %subtract_convert_fusion), channel_id=1, replica_groups=mesh['tm'=16,'sector'=8] {'tm'}, dimensions={0} | all-to-all | bytes 1638400 | tf_op jit(solution)/shard_map/all_to_all | solution.py:124
  (52 shorter events, 6.6 us)
Async XLA Ops:
  0.0 2.2 copy-start
  2.2 4.7 %copy-start.2 = (bf16[1,1,640,640]{3,2,1,0:T(8,128)(2,1)S(1)}, bf16[1,1,640,640]{3,2,1,0:T(8,128)(2,1)}, u32[]{:S(2)}) copy-start(bf16[1,1,640,640]{3,2,1,0:T(8,128)(2,1)} %param.10) | copy-start | bytes 2457604
  5.0 13.9 %collective-permute-start = (bf16[1,640,640]{2,1,0:T(8,128)(2,1)}, bf16[1,640,640]{2,1,0:T(8,128)(2,1)S(1)}, u32[]{:S(2)}, u32[]{:S(2)}) collective-permute-start(bf16[1,640,640]{2,1,0:T(8,128)(2,1)} %fusion.15), channel_id=1, source_target_pairs={{0,1},{1,2},{2,3},{3,4},{4,5},{5,6},{6,7},{8,9},{9,10},{10,11},{11... | collective-permute-start | bytes 2457608 | tf_op jit(solution)/shard_map/ppermute | solution.py:10
  7.2 13.5 %collective-permute-start.1 = (bf16[1,640,640]{2,1,0:T(8,128)(2,1)S(1)}, bf16[1,640,640]{2,1,0:T(8,128)(2,1)S(1)}, u32[]{:S(2)}, u32[]{:S(2)}) collective-permute-start(bf16[1,640,640]{2,1,0:T(8,128)(2,1)S(1)} %and_select_fusion.1), channel_id=1, source_target_pairs={{1,0},{2,1},{3,2},{4,3},{5,4},{6,5},{7,6},{9,8},{10,9},{11,10},{12... | collective-permute-start | bytes 2457608 | tf_op jit(solution)/shard_map/ppermute | solution.py:10
  18.9 1.9 copy-start.3
  25.0 16.2 %all-to-all-start = ((bf16[16,1,16,640]{3,2,1,0:T(8,128)(2,1)}), bf16[16,1,16,640]{3,2,1,0:T(8,128)(2,1)S(1)}, u32[]{:S(2)}, u32[]{:S(2)}) async-start(bf16[16,1,16,640]{3,2,1,0:T(8,128)(2,1)} %split.8), calls=%async_computation | async-start | bytes 655360 | tf_op jit(solution)/shard_map/all_to_all | solution.py:37
  63.4 232.7 %all-to-all-start.2 = ((bf16[16,1,640,640]{3,2,1,0:T(8,128)(2,1)}), bf16[16,1,640,640]{3,2,1,0:T(8,128)(2,1)}, u32[]{:S(2)}, u32[]{:S(2)}) async-start(bf16[16,1,640,640]{3,2,1,0:T(8,128)(2,1)} %stack.5), calls=%async_computation.2 | async-start | bytes 26214400 | tf_op jit(solution)/shard_map/all_to_all | solution.py:72
  435.7 22.4 %copy-start.1 = (bf16[1,640,640]{2,1,0:T(8,128)(2,1)S(1)}, bf16[1,640,640]{2,1,0:T(8,128)(2,1)}, u32[]{:S(2)}) copy-start(bf16[1,640,640]{2,1,0:T(8,128)(2,1)} %param.11) | copy-start | bytes 2457604
